TPU v7x, 32 devices: a whole 2x2x4 slice. The times are simulated.
32 devices in a mesh: groups: 2 (over x), row: 16 (over z, y, core).
Axes of the slice: x: 2, y: 2, z: 4, core: 2. Of those that a mesh axis runs over, the one named last changes fastest.
Arguments:
- homolog_embedding: bfloat16 [128, 256, 64], P('groups', 'row'), parts along dimension 0, may hold values from -6 to 6
- pair_state_tiles: bfloat16 [512, 256, 128], P(('groups', 'row')), parts along dimension 0, may hold values from -6 to 6
- alignment_mask: int32 [128, 256], P('groups', 'row'), parts along dimension 0, may hold values 0 or 1
- token_real_mask: int32 [512], P('groups'), parts along dimension 0, may hold values 0 or 1
- lineup_standardize_scaling: float32 [64], replicated, may hold values from 0.1 to 1.9
- former_factor_proj: bfloat16 [64, 32], replicated, may hold values from -0.75 to 0.75
- latter_factor_proj: bfloat16 [64, 32], replicated, may hold values from -0.75 to 0.75
- outer_output_weight: bfloat16 [1024, 128], replicated, may hold values from -0.1875 to 0.1875
- pair_norm_gain: float32 [128], replicated, may hold values from 0.1 to 1.9
- pair_logit_weight: float32 [128, 8], replicated
- content_vector_proj: bfloat16 [64, 256], replicated, may hold values from -0.75 to 0.75
- sigmoid_switch_proj: bfloat16 [64, 256], replicated, may hold values from -0.75 to 0.75
- final_result_proj: bfloat16 [256, 64], replicated, may hold values from -0.375 to 0.375
Outputs:
- alignment_updated: bfloat16 [128, 256, 64], P('groups', 'row'), parts along dimension 0
- pair_updated: bfloat16 [512, 256, 128], P(('groups', 'row')), parts along dimension 0
There are 2 independent parts, one for each index of `groups`. A program takes and returns all parts, laid end to end along the dimension named above; an argument that names none is the same for every part. Nothing has to cross between parts.
All inputs are finite; a program needn't handle non-finite values. No bound on the sum of `alignment_mask` on one device may be relied on, other than what follows from the above.
Results may differ from a plain program's by a relative error of at most 0.007.
Values may be sent and summed in bfloat16 or wider, within the bound.
A program may use at most 128 MiB of HBM per device.

v0:
```python
import jax
import jax.numpy as jnp
from jax import lax
from jax.sharding import PartitionSpec as P


def layer_normalize(inputs, gain):
    inputs = inputs.astype(jnp.float32)
    center = jnp.mean(inputs, axis=-1, keepdims=True)
    spread = jnp.mean((inputs - center) ** 2, axis=-1, keepdims=True)
    return (inputs - center) * lax.rsqrt(spread + 1e-05) * gain


def pair_terms(folded, local_mask, right_piece, mask_piece):
    product = jnp.einsum("seiz,sje->ijz", folded, right_piece, preferred_element_type=jnp.float32)
    counts = jnp.einsum("si,sj->ij", local_mask, mask_piece, preferred_element_type=jnp.float32)
    return product / (1.0 + counts)[:, :, None]


def shards(
    homolog_embedding,
    pair_state_tiles,
    alignment_mask,
    token_real_mask,
    lineup_standardize_scaling,
    former_factor_proj,
    latter_factor_proj,
    outer_output_weight,
    pair_norm_gain,
    pair_logit_weight,
    content_vector_proj,
    sigmoid_switch_proj,
    final_result_proj,
):
    normed_input = layer_normalize(homolog_embedding, lineup_standardize_scaling).astype(
        jnp.bfloat16
    )
    mask_halved = alignment_mask.astype(jnp.bfloat16)
    mask_float = mask_halved.astype(jnp.float32)
    left_rows = (
        jnp.dot(normed_input, former_factor_proj, preferred_element_type=jnp.float32)
        * mask_float[:, :, None]
    ).astype(jnp.bfloat16)
    factor = former_factor_proj.shape[1]
    channels = outer_output_weight.shape[1]
    weight_cube = outer_output_weight.reshape(factor, factor, channels)
    folded = jnp.einsum(
        "sic,cez->seiz", left_rows, weight_cube, preferred_element_type=jnp.float32
    ).astype(jnp.bfloat16)
    head_count = pair_logit_weight.shape[1]
    head_width = content_vector_proj.shape[1] // head_count
    gathered, gathered_mask = (
        lax.all_gather(normed_input, "row", axis=1, tiled=True),
        lax.all_gather(mask_halved, "row", axis=1, tiled=True),
    )
    right_all = (
        jnp.dot(gathered, latter_factor_proj, preferred_element_type=jnp.float32)
        * gathered_mask.astype(jnp.float32)[:, :, None]
    ).astype(jnp.bfloat16)
    update = pair_terms(folded, mask_halved, right_all, gathered_mask)
    pair_updated = (pair_state_tiles.astype(jnp.float32) + update).astype(jnp.bfloat16)
    pair_normed = layer_normalize(pair_updated, pair_norm_gain)
    logits = jnp.einsum(
        "ijc,ch->hij", pair_normed, pair_logit_weight, precision=lax.Precision.HIGHEST
    )
    logits = jnp.where(token_real_mask[None, None, :] == 1, logits, -1000000000.0)
    weights = jax.nn.softmax(logits, axis=2).astype(jnp.bfloat16)
    seq_count, local_tokens = (normed_input.shape[0], normed_input.shape[1])
    values_all = jnp.dot(gathered, content_vector_proj, preferred_element_type=jnp.float32).astype(
        jnp.bfloat16
    )
    span = values_all.shape[1]
    heads_piece = values_all.reshape(seq_count, span, head_count, head_width)
    term = jnp.einsum("hij,sjhc->sihc", weights, heads_piece, preferred_element_type=jnp.float32)
    average = term.reshape(seq_count, local_tokens, head_count * head_width)
    gate_vals = jax.nn.sigmoid(
        jnp.dot(normed_input, sigmoid_switch_proj, preferred_element_type=jnp.float32)
    )
    gated_output = (gate_vals * average).astype(jnp.bfloat16)
    update_alignment = jnp.dot(gated_output, final_result_proj, preferred_element_type=jnp.float32)
    alignment_updated = (homolog_embedding.astype(jnp.float32) + update_alignment).astype(
        jnp.bfloat16
    )
    return (alignment_updated, pair_updated)


def solution(mesh):
    placed = (
        P("groups", "row", None),
        P(("groups", "row"), None, None),
        P("groups", "row"),
        P("groups"),
        P(),
        P(),
        P(),
        P(),
        P(),
        P(),
        P(),
        P(),
        P(),
    )
    return jax.shard_map(
        shards,
        mesh=mesh,
        in_specs=placed,
        out_specs=(P("groups", "row", None), P(("groups", "row"), None, None)),
        check_vma=False,
    )
```

profile of v0, /device:TPU:0, one launch (start us, length us, event | category | flops | bytes accessed | tf_op | source)
XLA Modules:
  0.0 111.5 jit_solution(13931650329398912923)
XLA Ops:
  7.2 0.0 copy-start
  7.2 0.0 copy-start.3
  7.2 0.0 all-gather.2.cloned.1.call-start
  7.2 1.2 %convert_reduce_fusion.1 = f32[64,16]{1,0:T(8,128)S(1)} fusion(bf16[64,16,64]{2,1,0:T(8,128)(2,1)} %param.13), kind=kLoop, calls=%fused_computation.44 | loop fusion | flops 130048 | bytes 135168 | tf_op jit(solution)/shard_map/reduce_sum | solution.py:9
  8.4 1.3 %fusion.44 = f32[64,16]{1,0:T(8,128)S(1)} fusion(bf16[64,16,64]{2,1,0:T(8,128)(2,1)} %param.13, f32[64,16]{1,0:T(8,128)S(1)} %broadcast_multiply_fusion), kind=kLoop, calls=%fused_computation.47 | loop fusion | flops 261120 | bytes 139264 | tf_op jit(solution)/shard_map/reduce_sum | solution.py:10
  9.8 2.0 %fusion.46 = bf16[64,16,64]{2,1,0:T(8,128)(2,1)} fusion(bf16[64,16,64]{2,1,0:T(8,128)(2,1)} %param.13, f32[64]{0:T(128)} %param.17, f32[64,16]{1,0:T(8,128)S(1)} %add_rsqrt_fusion, f32[64,16]{1,0:T(8,128)S(1)} %broadcast_multiply_fusion), kind=kLoop, calls=%fused_computation.49 | loop fusion | flops 327680 | bytes 270592 | tf_op jit(solution)/shard_map/convert_element_type | solution.py:35
  11.8 0.0 all-gather.2.cloned.1.call-update
  11.8 0.7 fusion.62
  12.5 23.4 %all_gather.7 = bf16[64,256]{0,1:T(8,128)(2,1)S(1)} all-gather(bf16[64,16]{0,1:T(8,128)(2,1)S(1)} %get-tuple-element.11), channel_id=1, replica_groups=mesh['groups'=2,'row'=16] {'row'}, dimensions={1}, use_global_device_ids=true | all-gather | bytes 34816 | tf_op jit(solution)/shard_map/all_gather | solution.py:54
  35.9 0.1 copy.47
  36.0 1.5 %copy.46 = bf16[16,256,128]{1,2,0:T(8,128)(2,1)S(1)} copy(bf16[16,256,128]{2,1,0:T(8,128)(2,1)} %param.14) | data formatting | bytes 2097152 | tf_op args[1]
  37.5 0.7 broadcast_compare_fusion
  38.2 0.1 convolution_add_fusion.1
  38.3 0.0 copy-done.3
  38.3 0.0 copy-start.5
  38.3 6.0 %convert_bitcast_fusion = bf16[64,32,16,128]{3,0,1,2:T(8,128)(2,1)} fusion(bf16[32,32,128]{2,1,0:T(8,128)(2,1)S(1)} %bitcast.59, bf16[64,16,64]{2,1,0:T(8,128)(2,1)} %fusion.46, f32[64,16]{0,1:T(8,128)S(1)} %get-tuple-element.10, bf16[64,32]{0,1:T(8,128)(2,1)} %param.18), kind=kOutput, calls=%fused_computation.6 | convolution fusion | flops 276889600 | bytes 8790016 | tf_op jit(solution)/shard_map/sic,cez->seiz/dot_general | solution.py:47
  44.3 22.9 %all-gather.2.cloned.1.call-done = bf16[64,256,64]{2,1,0:T(8,128)(2,1)} async-done(((bf16[64,16,64]{2,1,0:T(8,128)(2,1)}), bf16[64,256,64]{2,1,0:T(8,128)(2,1)}) %all-gather.2.cloned.1.call-update) | async-done | bytes 2097168 | tf_op jit(solution)/shard_map/all_gather | solution.py:53
  67.2 0.0 copy-done.5
  67.2 3.7 %fusion.19 = bf16[64,256,32,1]{1,2,0,3:T(8,128)(2,1)S(1)} fusion(bf16[64,256,64]{2,1,0:T(8,128)(2,1)} %all-gather.2.cloned.1.call-done, f32[64,256]{1,0:T(8,128)S(1)} %convert_element_type.54, bf16[64,32]{0,1:T(8,128)(2,1)S(1)} %copy-done.5), kind=kOutput, calls=%fused_computation.20 | convolution fusion | flops 68157440 | bytes 3215360 | tf_op jit(solution)/shard_map/dot_general | solution.py:57
  70.9 0.0 copy-start.7
  70.9 0.0 copy-start.8
  70.9 11.0 %convert_reduce_fusion = (f32[16,256]{1,0:T(8,128)S(1)}, bf16[16,256,128]{1,2,0:T(8,128)(2,1)S(1)}) fusion(f32[16,256]{1,0:T(8,128)S(1)} %convolution_add_fusion.1, bf16[64,256,32,1]{1,2,0,3:T(8,128)(2,1)S(1)} %fusion.19, bf16[64,32,16,128]{3,0,1,2:T(8,128)(2,1)} %convert_bitcast_fusion, bf16[16,256,128]{1,2,0:T(8,128)(2,1)S(1)} %copy.46), kind=kOutput, calls=%fused_computation.9 | convolution fusion | flops 2150625280 | bytes 11567104 | tf_op jit(solution)/shard_map/seiz,sje->ijz/dot_general | solution.py:15
  82.0 1.3 %copy.57 = bf16[16,256,128]{2,1,0:T(8,128)(2,1)} copy(bf16[16,256,128]{1,2,0:T(8,128)(2,1)S(1)} %get-tuple-element.13) | data formatting | bytes 2097152
  83.3 0.3 fusion.11
  83.6 0.0 copy-done.7
  83.6 0.0 copy-done.8
  83.7 1.5 %fusion.34 = f32[8,16,256]{2,0,1:T(8,128)S(1)} fusion(bf16[16,256,128]{1,2,0:T(8,128)(2,1)S(1)} %get-tuple-element.13, f32[128]{0:T(128)S(1)} %copy-done.8, f32[16,256]{1,0:T(8,128)S(1)} %add_rsqrt_fusion.1, f32[16,256]{1,0:T(8,128)S(1)} %broadcast_multiply_fusion.1, pred[256]{0:T(512)(128)(4,1)S(1)} %broadcast_compare_fusion, f32[128,8]{0,1:T(8,128)S(1)} %copy-done.7), kind=kOutput, calls=%fused_computation.36 | convolution fusion | flops 52461568 | bytes 1217280 | tf_op jit(solution)/shard_map/ijc,ch->hij/dot_general | solution.py:63
  85.1 0.2 fusion.38
  85.3 0.0 copy-done
  85.3 4.5 %convolution_convert_fusion = bf16[64,256,256]{1,2,0:T(8,128)(2,1)S(1)} fusion(bf16[64,256,64]{2,1,0:T(8,128)(2,1)} %all-gather.2.cloned.1.call-done, bf16[64,256]{1,0:T(8,128)(2,1)S(1)} %copy-done), kind=kOutput, calls=%fused_computation.7 | convolution fusion | flops 541065216 | bytes 10518528 | tf_op jit(solution)/shard_map/dot_general | solution.py:69
  89.9 7.5 %fusion.8 = f32[64,16,8,32]{3,1,0,2:T(8,128)} fusion(bf16[64,256,8,32]{1,3,2,0:T(8,128)(2,1)S(1)} %bitcast.57, bf16[8,16,256,1]{2,0,1,3:T(8,128)(2,1)S(1)} %fusion.38), kind=kOutput, calls=%fused_computation.12 | convolution fusion | flops 134217728 | bytes 9502720 | tf_op jit(solution)/shard_map/hij,sjhc->sihc/dot_general | solution.py:74
  97.4 0.0 copy-start.2
  97.4 0.0 copy-start.6
  97.4 2.9 %copy.54 = f32[64,16,8,32]{0,3,2,1:T(8,128)S(1)} copy(f32[64,16,8,32]{3,1,0,2:T(8,128)} %fusion.8) | data formatting | bytes 2097152 | tf_op jit(solution)/shard_map/hij,sjhc->sihc/transpose | solution.py:74
  100.3 0.0 copy-start.1
  100.3 0.0 copy-start.4
  100.3 1.6 %copy.55 = f32[64,16,256]{2,0,1:T(8,128)} copy(f32[64,16,256]{0,2,1:T(8,128)S(1)} %bitcast.58) | data formatting | bytes 2097152 | tf_op jit(solution)/shard_map/reshape | solution.py:75
  101.9 0.0 copy-done.2
  101.9 0.0 copy-done.6
  101.9 1.6 %fusion.24 = bf16[64,16,256]{2,0,1:T(8,128)(2,1)S(1)} fusion(f32[64,16,256]{2,0,1:T(8,128)} %copy.55, bf16[64,16,64]{2,1,0:T(8,128)(2,1)S(1)} %copy-done.2, bf16[64,256]{1,0:T(8,128)(2,1)S(1)} %copy-done.6), kind=kOutput, calls=%fused_computation.26 | convolution fusion | flops 34865152 | bytes 1736704 | tf_op jit(solution)/shard_map/dot_general | solution.py:77
  103.5 0.0 copy-done.1
  103.6 0.0 copy-done.4
  103.6 1.1 %fusion.25 = bf16[64,16,64]{2,1,0:T(8,128)(2,1)} fusion(bf16[64,16,64]{2,1,0:T(8,128)(2,1)S(1)} %copy-done.1, bf16[64,16,256]{2,0,1:T(8,128)(2,1)S(1)} %fusion.24, bf16[256,64]{0,1:T(8,128)(2,1)S(1)} %copy-done.4), kind=kOutput, calls=%fused_computation.28 | convolution fusion | flops 33751040 | bytes 819200 | tf_op jit(solution)/shard_map/dot_general | solution.py:80
  (5 shorter events, 0.0 us)
Async XLA Ops:
  7.2 78.2 %copy-start = (bf16[64,256]{1,0:T(8,128)(2,1)S(1)}, bf16[64,256]{1,0:T(8,128)(2,1)}, u32[]{:S(2)}) copy-start(bf16[64,256]{1,0:T(8,128)(2,1)} %param.23) | copy-start | bytes 98308
  7.2 31.1 %copy-start.3 = (bf16[1024,128]{1,0:T(8,128)(2,1)S(1)}, bf16[1024,128]{1,0:T(8,128)(2,1)}, u32[]{:S(2)}) copy-start(bf16[1024,128]{1,0:T(8,128)(2,1)} %param.20) | copy-start | bytes 786436
  7.2 60.0 %all-gather.2.cloned.1.call-start = ((), (), s32[]{:S(2)}) async-start(), calls=%async_computation | async-start | bytes 4456448 | tf_op jit(solution)/shard_map/all_gather | solution.py:53
  38.3 28.9 %copy-start.5 = (bf16[64,32]{0,1:T(8,128)(2,1)S(1)}, bf16[64,32]{0,1:T(8,128)(2,1)}, u32[]{:S(2)}) copy-start(bf16[64,32]{0,1:T(8,128)(2,1)} %param.19) | copy-start | bytes 12292
  70.9 12.7 %copy-start.7 = (f32[128,8]{0,1:T(8,128)S(1)}, f32[128,8]{0,1:T(8,128)}, u32[]{:S(2)}) copy-start(f32[128,8]{0,1:T(8,128)} %param.22) | copy-start | bytes 12292
  70.9 12.7 %copy-start.8 = (f32[128]{0:T(128)S(1)}, f32[128]{0:T(128)}, u32[]{:S(2)}) copy-start(f32[128]{0:T(128)} %param.21) | copy-start | bytes 1540
  97.4 4.5 %copy-start.2 = (bf16[64,16,64]{2,1,0:T(8,128)(2,1)S(1)}, bf16[64,16,64]{2,1,0:T(8,128)(2,1)}, u32[]{:S(2)}) copy-start(bf16[64,16,64]{2,1,0:T(8,128)(2,1)} %fusion.46) | copy-start | bytes 393220
  97.4 4.5 %copy-start.6 = (bf16[64,256]{1,0:T(8,128)(2,1)S(1)}, bf16[64,256]{1,0:T(8,128)(2,1)}, u32[]{:S(2)}) copy-start(bf16[64,256]{1,0:T(8,128)(2,1)} %param.24) | copy-start | bytes 98308
  100.3 3.3 %copy-start.1 = (bf16[64,16,64]{2,1,0:T(8,128)(2,1)S(1)}, bf16[64,16,64]{2,1,0:T(8,128)(2,1)}, u32[]{:S(2)}) copy-start(bf16[64,16,64]{2,1,0:T(8,128)(2,1)} %param.13) | copy-start | bytes 393220
  100.3 3.3 %copy-start.4 = (bf16[256,64]{0,1:T(8,128)(2,1)S(1)}, bf16[256,64]{0,1:T(8,128)(2,1)}, u32[]{:S(2)}) copy-start(bf16[256,64]{0,1:T(8,128)(2,1)} %param.25) | copy-start | bytes 98308
Sparse Core Ops, SparseCore 0:
  11.9 55.2 all-gather.1
where the time goes:
time: 112 us
  matrix products  37.2 us (33%)
  blocking collectives  23.4 us (21%)
  waiting for transfers between devices  22.9 us (20%)
  between operations  14.2 us (13%)
  local copies, waits for them, and re-layouts  7.38 us (7%)
  other arithmetic  6.42 us (6%)
    all_gather x1, blocking collectives, shards(): lax.all_gather(mask_halved, 'row', axis=1, tiled=True)  23.4 us
    all_gather x1, waiting for transfers between devices, shards(): lax.all_gather(normed_input, 'row', axis=1, tiled=True)  22.9 us
    dot_general x1, matrix products, pair_terms(): jnp.einsum('seiz,sje->ijz', folded, right_piece, preferred_element_type=j...  11 us
    dot_general x1, matrix products, shards(): jnp.einsum('hij,sjhc->sihc', weights, heads_piece, preferred_element_type...  7.5 us
    dot_general x1, matrix products, shards(): jnp.einsum('sic,cez->seiz', left_rows, weight_cube, preferred_element_typ...  5.96 us
    dot_general x1, matrix products, shards(): jnp.dot(gathered, content_vector_proj, preferred_element_type=jnp.float32)  4.55 us
    dot_general x1, matrix products, shards(): jnp.dot(gathered, latter_factor_proj, preferred_element_type=jnp.float32)  3.72 us
    transpose x1, local copies, waits for them, and re-layouts, shards(): jnp.einsum('hij,sjhc->sihc', weights, heads_piece, preferred_element_type...  2.87 us
  transfers between devices with their start and end apart: 1, of which 1 were waited for; matrix products, arithmetic and copies ran while one was open for 8% of the time, Pallas kernels for 0%

commit v1 on v0

v1 whole, which is shorter than its diff:
```python
import functools

import jax
import jax.numpy as jnp
from jax import lax
from jax.experimental import pallas as pl
from jax.experimental.pallas import tpu as pltpu
from jax.sharding import PartitionSpec as P

F32 = jnp.float32
BF = jnp.bfloat16
MESH = pl.DeviceIdType.MESH
NT = (((1,), (1,)), ((), ()))


def mm(a, b):
    return jnp.dot(a, b, preferred_element_type=F32)


def iota(shape, dim):
    return lax.broadcasted_iota(jnp.int32, shape, dim)


def kernel(
    dims,
    x_ref, pair_hbm, mask_ref, tok_ref, scale_ref, former_ref, latter_ref, outw_ref,
    gain_ref, logitw_ref, content_ref, switch_ref, final_ref,
    out_ref, pair_out_hbm,
    gr, gn, fold, n2_sc, lhs_sc, rt_sc, wf_sc, wl_sc, mr_sc, gw_sc, lg_sc, bd_sc, fin_sc,
    gate_sc, a2_sc, pair_in, pair_new,
    r_recv, rz_send, ry_send, rp_send, n_recv, nz_send, ny_send, np_send, in_sem, out_sem,
):
    nz, chunks = dims
    seqs, loc, feat = x_ref.shape
    half = seqs // 2
    lanes = 2 * feat
    pairs = loc // 2
    factor = former_ref.shape[1]
    zdim = outw_ref.shape[1]
    heads = logitw_ref.shape[1]
    width = content_ref.shape[1] // heads
    span = gn.shape[1]
    tiles = factor * seqs // 128
    per = half // chunks
    half_rows = half * loc

    group = lax.axis_index("groups")
    me = lax.axis_index("row")
    core = lax.rem(me, 2)
    yy = lax.rem(me // 2, 2)
    zz = me // 4

    def dev(z, y, c):
        return (z * 2 + y) * 2 + c

    def far(dz):
        return lax.rem(zz + dz, nz)

    partner = dev(zz, yy, 1 - core)
    yside = dev(zz, 1 - yy, core)

    barrier = pltpu.get_barrier_semaphore()
    peers = [dev(far(dz), yy, core) for dz in range(1, nz)] + [yside, partner]
    for peer in peers:
        pl.semaphore_signal(barrier, inc=1, device_id=(group, peer), device_id_type=MESH)

    load = pltpu.make_async_copy(pair_hbm, pair_in, in_sem)
    load.start()

    def rows_of(d):
        return pl.ds(pl.multiple_of(d * loc, loc), loc)

    def r_copy(d, target, sem):
        view = gr.at[:, rows_of(d), :]
        return pltpu.make_async_remote_copy(
            src_ref=view, dst_ref=view, send_sem=sem, recv_sem=r_recv.at[d],
            device_id=(group, target), device_id_type=MESH)

    def n_copy(ch, d, target, sem):
        view = gn.at[pl.ds(ch * per, per), rows_of(d), :]
        return pltpu.make_async_remote_copy(
            src_ref=view, dst_ref=view, send_sem=sem, recv_sem=n_recv.at[ch, d],
            device_id=(group, target), device_id_type=MESH)

    x = x_ref[...].astype(F32)
    center = jnp.mean(x, axis=-1, keepdims=True)
    spread = jnp.mean((x - center) ** 2, axis=-1, keepdims=True)
    normed = ((x - center) * lax.rsqrt(spread + 1e-05) * scale_ref[...][None]).astype(BF).astype(F32)
    n2 = jnp.concatenate(
        [normed[:half].reshape(half_rows, feat), normed[half:].reshape(half_rows, feat)], axis=1)
    n2_sc[...] = n2
    own = rows_of(me)
    gn[:, own, :] = n2.astype(BF).reshape(half, loc, lanes)

    mask = mask_ref[...].astype(F32)
    mask_pad = jnp.concatenate([mask, jnp.zeros((seqs, 128 - loc), F32)], axis=1)
    mask_sq = jnp.concatenate([mask_pad, jnp.zeros((128 - seqs, 128), F32)], axis=0)
    gr[tiles, own, :] = mask_sq.T[:loc].astype(BF)
    proj = jnp.concatenate(
        [former_ref[...].astype(F32), latter_ref[...].astype(F32),
         jnp.zeros((feat, 128 - 2 * factor), F32)], axis=1).astype(BF)

    def rows_for(i):
        packed = n2_sc[pl.ds(i, half, stride=loc), :]
        rows = jnp.concatenate([packed[:, :feat], packed[:, feat:]], axis=0)
        return rows * mask[:, i:i + 1]

    for i2 in range(pairs):
        rows = jnp.concatenate([rows_for(i2), rows_for(i2 + pairs)], axis=0).astype(BF)
        both = mm(rows, proj)
        lhs_sc[i2] = both.astype(BF)
        flipped = both.T
        rt_sc[pl.ds(i2 * factor, factor), :] = flipped[factor:2 * factor]
    low = iota((pairs, 128), 1) < seqs
    for t in range(tiles):
        a = rt_sc[pl.ds(2 * t, pairs, stride=factor), :]
        b = rt_sc[pl.ds(2 * t + 1, pairs, stride=factor), :]
        top = jnp.where(low, a, pltpu.roll(b, seqs, 1))
        bottom = jnp.where(low, pltpu.roll(a, seqs, 1), b)
        gr[t, own, :] = jnp.concatenate([top, bottom], axis=0).astype(BF)

    wf_sc[...] = outw_ref[...].astype(F32)
    for e in range(factor):
        wl_sc[:, e * zdim:(e + 1) * zdim] = wf_sc[pl.ds(e, factor, stride=factor), :].astype(BF)

    pl.semaphore_wait(barrier, nz + 1)
    r_copy(me, yside, ry_send.at[0]).start()
    for dz in range(1, nz):
        r_copy(me, dev(far(dz), yy, core), rz_send.at[dz]).start()
    r_copy(me, partner, rp_send.at[0, 0]).start()
    for ch in range(chunks):
        for dz in range(1, nz):
            n_copy(ch, me, dev(far(dz), yy, core), nz_send.at[ch, dz]).start()

    stride = max(1, pairs // nz)

    def r_relay(dz):
        d = dev(far(dz), yy, core)
        r_copy(d, partner, ry_send.at[dz]).wait_recv()
        r_copy(d, yside, ry_send.at[dz]).start()
        r_copy(d, partner, rp_send.at[0, dz]).start()

    def fold_step(i2, carry):
        left = lhs_sc[i2][:, :factor]
        step = 8
        for e0 in range(0, factor, step):
            res = mm(left, wl_sc[:, e0 * zdim:(e0 + step) * zdim]).astype(BF)
            for e in range(e0, e0 + step):
                part = res[:, (e - e0) * zdim:(e - e0 + 1) * zdim]
                fold[i2, e * seqs:(e + 1) * seqs, :zdim] = part[:seqs]
                fold[i2, e * seqs:(e + 1) * seqs, zdim:] = part[seqs:]
        dz = (i2 + 1) // stride - 1

        @pl.when((lax.rem(i2 + 1, stride) == 0) & (dz >= 1) & (dz < nz))
        def _():
            r_relay(dz)

        return carry

    lax.fori_loop(0, pairs, fold_step, 0)
    for dz in range(max(1, pairs // stride), nz):
        r_relay(dz)
    for ch in range(chunks):
        n_copy(ch, me, yside, ny_send.at[ch, 0]).start()

    for i2 in range(pairs):
        for k in range(2):
            col = mask_sq[:, i2 + k * pairs:i2 + k * pairs + 1]
            mr_sc[i2, :, k * zdim:(k + 1) * zdim] = jnp.broadcast_to(col, (128, zdim)).astype(BF)
    lw = jnp.concatenate([logitw_ref[...], jnp.zeros((zdim, 128 - heads), F32)], axis=1).T[:heads]
    gw = lw * gain_ref[...]
    g0 = gw.astype(BF).astype(F32)
    g1 = (gw - g0).astype(BF).astype(F32)
    g2 = gw - g0 - g1
    flat = jnp.concatenate([g0, g1, g2, jnp.zeros((heads, zdim), F32)], axis=0)
    ones = jnp.concatenate([jnp.zeros((3 * heads, zdim), F32), jnp.ones((heads, zdim), F32)], axis=0)
    gw_sc[...] = jnp.concatenate([flat, flat, ones, ones], axis=1).astype(BF)

    cols = heads * 2 * width
    pick = (iota((heads * width, cols), 0)
            == (iota((heads * width, cols), 1) // (2 * width)) * width
            + iota((heads * width, cols), 1) % width).astype(F32).astype(BF)
    content = mm(content_ref[...], pick)
    wide = cols // 2
    for g in range(2):
        part = jnp.concatenate([content[:, g * wide:(g + 1) * wide]] * heads, axis=0)
        keep = iota(part.shape, 0) // feat == iota(part.shape, 1) // width
        bd_sc[g] = jnp.where(keep, part, 0.0).astype(BF)
    switch = mm(switch_ref[...], pick)
    switch = jnp.concatenate([switch, switch], axis=0)
    keep = iota(switch.shape, 0) // feat == (iota(switch.shape, 1) // width) % 2
    switch = jnp.where(keep, switch, 0.0).astype(BF)
    fin = final_ref[...].astype(F32)
    blocks = []
    for h in range(heads):
        blocks += [fin[h * width:(h + 1) * width]] * 2
    fin = jnp.concatenate(blocks, axis=0)
    fin = jnp.concatenate([fin, fin], axis=1)
    keep = (iota(fin.shape, 0) // width) % 2 == iota(fin.shape, 1) // feat
    fin_sc[...] = jnp.where(keep, fin, 0.0).astype(BF)

    for q in range(4):
        size = half_rows // 4
        pre = mm(n2_sc[q * size:(q + 1) * size, :].astype(BF), switch)
        gate_sc[q * size:(q + 1) * size, :] = jax.nn.sigmoid(pre)

    for dz in range(nz):
        d = dev(far(dz), 1 - yy, core)
        r_copy(d, partner, rp_send.at[1, dz]).wait_recv()
        r_copy(d, partner, rp_send.at[1, dz]).start()
    for ch in range(chunks):
        n_copy(ch, me, partner, np_send.at[ch, 0, 0]).start()
    for y in range(2):
        for dz in range(nz):
            d = dev(far(dz), lax.rem(yy + y, 2), 1 - core)
            r_copy(d, partner, rp_send.at[y, dz]).wait_recv()
    load.wait()

    real = tok_ref[...] == 1
    mean_of = jnp.full((zdim, zdim), 1.0 / zdim, F32).astype(BF)
    rel = pairs // chunks

    def pair_step(i2, carry):
        lhs = jnp.concatenate([gr[t] for t in range(tiles)], axis=1)
        acc = mm(lhs, fold[i2])
        counts = mm(gr[tiles], mr_sc[i2])
        acc = acc / (1.0 + counts)
        for k in range(2):
            i = i2 + k * pairs
            new = (pair_in[i].astype(F32) + acc[:, k * zdim:(k + 1) * zdim]).astype(BF)
            pair_new[i] = new
            cent = new.astype(F32) - mm(new, mean_of)
            hi = cent.astype(BF)
            lo = (cent - hi.astype(F32)).astype(BF)
            sq = cent * cent
            sh = sq.astype(BF)
            sl = (sq - sh.astype(F32)).astype(BF)
            rhs = jnp.concatenate([hi, lo, sh, sl], axis=1)
            res = lax.dot_general(gw_sc[...], rhs, NT, preferred_element_type=F32)
            total = res[:heads] + res[heads:2 * heads] + res[2 * heads:3 * heads]
            logits = total * lax.rsqrt(res[3 * heads:] / zdim + 1e-05)
            logits = jnp.where(real, logits, -1000000000.0)
            for t in range(span // 128):
                lg_sc[t, pl.ds(i, heads, stride=loc), :] = logits[:, t * 128:(t + 1) * 128]
        ch = i2 // rel

        @pl.when(lax.rem(i2, rel) == 0)
        def _():
            for dz in range(1, nz):
                d = dev(far(dz), yy, core)
                n_copy(ch, d, yside, ny_send.at[ch, dz]).wait_recv()
                n_copy(ch, d, yside, ny_send.at[ch, dz]).start()
                n_copy(ch, d, partner, np_send.at[ch, 0, dz]).start()

        @pl.when(lax.rem(i2, rel) == rel - 1)
        def _():
            for dz in range(nz):
                d = dev(far(dz), 1 - yy, core)
                n_copy(ch, d, partner, np_send.at[ch, 1, dz]).wait_recv()
                n_copy(ch, d, partner, np_send.at[ch, 1, dz]).start()

        return carry

    lax.fori_loop(0, pairs, pair_step, 0)
    save = pltpu.make_async_copy(pair_new, pair_out_hbm, out_sem)
    save.start()

    logits = jnp.concatenate([lg_sc[t] for t in range(span // 128)], axis=1)
    top = jnp.max(logits, axis=1, keepdims=True)
    raised = jnp.exp(logits - top)
    weights = (raised / jnp.sum(raised, axis=1, keepdims=True)).astype(BF)

    def average_chunk(ch, carry):
        for y in range(2):
            for dz in range(nz):
                d = dev(far(dz), lax.rem(yy + y, 2), 1 - core)
                n_copy(ch, d, partner, np_send.at[ch, y, dz]).wait_recv()
        for q in range(0, per, 2):
            p = ch * per + q
            rhs = jnp.concatenate([gn[p], gn[p + 1]], axis=1)
            res = mm(weights, rhs).astype(BF)
            for k in range(2):
                at = pl.ds(pl.multiple_of((p + k) * loc, loc), loc)
                for h in range(heads):
                    a2_sc[at, h * lanes:(h + 1) * lanes] = (
                        res[h * loc:(h + 1) * loc, k * lanes:(k + 1) * lanes])
        size = per * loc
        at = pl.ds(pl.multiple_of(ch * size, size), size)
        total = jnp.zeros((size, lanes), F32)
        rows = heads * lanes // 2
        for g in range(2):
            mean = mm(a2_sc[at, g * rows:(g + 1) * rows], bd_sc[g])
            gated = (gate_sc[at, g * wide:(g + 1) * wide] * mean).astype(BF)
            total += mm(gated, fin_sc[g * wide:(g + 1) * wide, :])
        for k in range(2):
            where = pl.ds(ch * per + k * half, per)
            piece = total[:, k * feat:(k + 1) * feat].reshape(per, loc, feat)
            out_ref[where] = (x_ref[where].astype(F32) + piece).astype(BF)
        return carry

    lax.fori_loop(0, chunks, average_chunk, 0)

    for dz in range(nz):
        if dz:
            r_copy(me, yside, rz_send.at[dz]).wait_send()
        r_copy(me, yside, ry_send.at[dz]).wait_send()
        for y in range(2):
            r_copy(me, yside, rp_send.at[y, dz]).wait_send()

    def drain(ch, carry):
        for dz in range(nz):
            if dz:
                n_copy(ch, me, yside, nz_send.at[ch, dz]).wait_send()
            n_copy(ch, me, yside, ny_send.at[ch, dz]).wait_send()
            for y in range(2):
                n_copy(ch, me, yside, np_send.at[ch, y, dz]).wait_send()
        return carry

    lax.fori_loop(0, chunks, drain, 0)
    save.wait()


def shards(row_count, x, pair, mask, tok, scale, former, latter, outw, gain, logitw, content, switch, final):
    seqs, loc, feat = x.shape
    span, zdim = pair.shape[1:]
    factor = former.shape[1]
    heads = logitw.shape[1]
    width = content.shape[1] // heads
    nz = row_count // 4
    chunks = 4
    half = seqs // 2
    lanes = 2 * feat
    pairs = loc // 2
    tiles = factor * seqs // 128
    vm = pl.BlockSpec(memory_space=pltpu.VMEM)
    hbm = pl.BlockSpec(memory_space=pl.ANY)
    dma = pltpu.SemaphoreType.DMA
    return pl.pallas_call(
        functools.partial(kernel, (nz, chunks)),
        out_shape=(jax.ShapeDtypeStruct(x.shape, x.dtype), jax.ShapeDtypeStruct(pair.shape, pair.dtype)),
        in_specs=[vm, hbm] + [vm] * 11,
        out_specs=(vm, hbm),
        scratch_shapes=[
            pltpu.VMEM((tiles + 1, span, 128), BF),
            pltpu.VMEM((half, span, lanes), BF),
            pltpu.VMEM((pairs, factor * seqs, 2 * zdim), BF),
            pltpu.VMEM((half * loc, lanes), F32),
            pltpu.VMEM((pairs, 2 * seqs, 128), BF),
            pltpu.VMEM((pairs * factor, 128), F32),
            pltpu.VMEM((factor * factor, zdim), F32),
            pltpu.VMEM((factor, factor * zdim), BF),
            pltpu.VMEM((pairs, 128, 2 * zdim), BF),
            pltpu.VMEM((4 * heads, 4 * zdim), BF),
            pltpu.VMEM((span // 128, heads * loc, 128), F32),
            pltpu.VMEM((2, heads * lanes // 2, heads * width), BF),
            pltpu.VMEM((2 * heads * width, lanes), BF),
            pltpu.VMEM((half * loc, 2 * heads * width), F32),
            pltpu.VMEM((half * loc, heads * lanes), BF),
            pltpu.VMEM((loc, span, zdim), BF),
            pltpu.VMEM((loc, span, zdim), BF),
            dma((row_count,)),
            dma((nz,)),
            dma((nz,)),
            dma((2, nz)),
            dma((chunks, row_count)),
            dma((chunks, nz)),
            dma((chunks, nz)),
            dma((chunks, 2, nz)),
            dma,
            dma,
        ],
        compiler_params=pltpu.CompilerParams(
            collective_id=0, has_side_effects=True, vmem_limit_bytes=60 * 1024 * 1024),
        name="msa_step",
    )(x, pair, mask, tok.reshape(1, span), scale.reshape(1, feat), former, latter, outw,
      gain.reshape(1, zdim), logitw, content, switch, final)


def solution(mesh):
    placed = (
        P("groups", "row", None),
        P(("groups", "row"), None, None),
        P("groups", "row"),
        P("groups"),
    ) + (P(),) * 9
    return jax.shard_map(
        functools.partial(shards, mesh.shape["row"]),
        mesh=mesh,
        in_specs=placed,
        out_specs=(P("groups", "row", None), P(("groups", "row"), None, None)),
        check_vma=False,
    )
```

time: 112 us -> 55.9 us (0.50)
  the two profiles are of different devices: /device:TPU:0 before, /device:TPU:10 now
where the time goes in v1:
time: 55.9 us; the launch traced here: 55.6 us
  Pallas kernels  46.7 us (84%)
  local copies, waits for them, and re-layouts  8.24 us (15%)
  between operations  0.65 us (1%)
    pallas_call x1, Pallas kernels, shards(): pl.pallas_call(functools.partial(kernel, (nz, chunks)), out_shape=(jax.Sh...  46.7 us
    unnamed x15, local copies, waits for them, and re-layouts  8.24 us

profile of v1, /device:TPU:10, one launch (start us, length us, event | category | flops | bytes accessed | tf_op | source)
XLA Modules:
  0.0 55.6 jit_solution(7942901881429217145)
XLA Ops:
  0.6 0.0 copy-start.1
  0.6 1.4 %copy.16.former_ref = bf16[64,32]{1,0:T(8,128)(2,1)} copy(bf16[64,32]{0,1:T(8,128)(2,1)} %param.18) | data formatting | bytes 8192 | tf_op args[5]
  2.0 0.0 copy-done.1
  2.0 0.0 copy-start.2
  2.0 0.7 %copy.17.latter_ref = bf16[64,32]{1,0:T(8,128)(2,1)} copy(bf16[64,32]{0,1:T(8,128)(2,1)S(1)} %copy-done.1) | data formatting | bytes 8192 | tf_op args[6]
  2.7 0.0 copy-done.2
  2.7 0.0 copy-start.3
  2.7 0.7 %copy.15.mask_ref = s32[64,16]{1,0:T(8,128)} copy(s32[64,16]{0,1:T(8,128)S(1)} %copy-done.2) | data formatting | bytes 8192 | tf_op args[2]
  3.4 0.0 copy-done.3
  3.4 0.0 copy-start
  3.4 0.7 %copy.18.logitw_ref = f32[128,8]{1,0:T(8,128)} copy(f32[128,8]{0,1:T(8,128)S(1)} %copy-done.3) | data formatting | bytes 8192 | tf_op args[9]
  4.2 0.0 copy-done
  4.2 0.7 %copy.19.final_ref = bf16[256,64]{1,0:T(8,128)(2,1)} copy(bf16[256,64]{0,1:T(8,128)(2,1)S(1)} %copy-done) | data formatting | bytes 65536 | tf_op args[12]
  4.9 46.7 %msa_step.1 = (bf16[64,16,64]{2,1,0:T(8,128)(2,1)}, bf16[16,256,128]{2,1,0:T(8,128)(2,1)}) custom-call(bf16[64,16,64]{2,1,0:T(8,128)(2,1)} %x_ref.1, bf16[16,256,128]{2,1,0:T(8,128)(2,1)} %pair_hbm.1, s32[64,16]{1,0:T(8,128)} %copy.15.mask_ref, s32[1,256]{1,0:T(1,128)} %bitcast.3, f32[1,64]{1,0:T(1,128)} %bitcast.4, bf16[64,32]{1,0:T(8,128)(2,1)} %copy.16.former_ref, ...), custom_call_target="tpu_custom_call" | custom-call | tf_op jit(solution)/shard_map/msa_step/pallas_call | solution.py:338
  51.6 1.7 %copy.22 = bf16[64,16,64]{2,1,0:T(8,128)(2,1)} copy(bf16[64,16,64]{2,1,0:T(8,128)(2,1)} %get-tuple-element.4) | data formatting | bytes 262144
  53.3 2.3 %copy.23 = bf16[16,256,128]{2,1,0:T(8,128)(2,1)} copy(bf16[16,256,128]{2,1,0:T(8,128)(2,1)} %get-tuple-element.5) | data formatting | bytes 2097152
Async XLA Ops:
  0.6 1.4 %copy-start.1 = (bf16[64,32]{0,1:T(8,128)(2,1)S(1)}, bf16[64,32]{0,1:T(8,128)(2,1)}, u32[]{:S(2)}) copy-start(bf16[64,32]{0,1:T(8,128)(2,1)} %param.19) | copy-start | bytes 12292
  2.0 0.7 %copy-start.2 = (s32[64,16]{0,1:T(8,128)S(1)}, s32[64,16]{0,1:T(8,128)}, u32[]{:S(2)}) copy-start(s32[64,16]{0,1:T(8,128)} %param.15) | copy-start | bytes 12292
  2.7 0.7 %copy-start.3 = (f32[128,8]{0,1:T(8,128)S(1)}, f32[128,8]{0,1:T(8,128)}, u32[]{:S(2)}) copy-start(f32[128,8]{0,1:T(8,128)} %param.22) | copy-start | bytes 12292
  3.4 0.8 %copy-start = (bf16[256,64]{0,1:T(8,128)(2,1)S(1)}, bf16[256,64]{0,1:T(8,128)(2,1)}, u32[]{:S(2)}) copy-start(bf16[256,64]{0,1:T(8,128)(2,1)} %param.25) | copy-start | bytes 98308

commit v2 on v1

--- a/solution.py
+++ b/solution.py
@@ -23,23 +23,30 @@
 
 def kernel(
     dims,
-    x_ref, pair_hbm, mask_ref, tok_ref, scale_ref, former_ref, latter_ref, outw_ref,
-    gain_ref, logitw_ref, content_ref, switch_ref, final_ref,
-    out_ref, pair_out_hbm,
-    gr, gn, fold, n2_sc, lhs_sc, rt_sc, wf_sc, wl_sc, mr_sc, gw_sc, lg_sc, bd_sc, fin_sc,
-    gate_sc, a2_sc, pair_in, pair_new,
-    r_recv, rz_send, ry_send, rp_send, n_recv, nz_send, ny_send, np_send, in_sem, out_sem,
+    *refs,
 ):
+    count = 13
+    sources, held = refs[:count], refs[count + 2:2 * count + 2]
+    (x_ref, pair_in, mask_ref, tok_ref, scale_ref, former_ref, latter_ref, outw_ref,
+     gain_ref, logitw_ref, content_ref, switch_ref, final_ref) = held
+    out_ref, pair_new = refs[count:count + 2]
+    (gr, gn, fold, n2_sc, lhs_sc, rt_sc, wf_sc, wl_sc, mr_sc, gw_sc, lg_sc, bd_sc, fin_sc,
+    gate_sc, a2_sc,
+    r_recv, rz_send, ry_send, rp_send, n_recv, nz_send, ny_send, np_send, in_sem) = refs[2 * count + 2:]
+    loads = [pltpu.make_async_copy(a, b, in_sem.at[k]) for k, (a, b) in enumerate(zip(sources, held))]
+    order = (0, 4, 2, 5, 6, 7, 9, 8, 10, 11, 12, 3, 1)
+    for k in order:
+        loads[k].start()
     nz, chunks = dims
     seqs, loc, feat = x_ref.shape
     half = seqs // 2
     lanes = 2 * feat
     pairs = loc // 2
-    factor = former_ref.shape[1]
+    factor = former_ref.shape[0]
     zdim = outw_ref.shape[1]
-    heads = logitw_ref.shape[1]
+    heads = logitw_ref.shape[0]
     width = content_ref.shape[1] // heads
-    span = gn.shape[1]
+    span = gn.shape[1] * loc
     tiles = factor * seqs // 128
     per = half // chunks
     half_rows = half * loc
@@ -64,24 +71,21 @@
     for peer in peers:
         pl.semaphore_signal(barrier, inc=1, device_id=(group, peer), device_id_type=MESH)
 
-    load = pltpu.make_async_copy(pair_hbm, pair_in, in_sem)
-    load.start()
-
-    def rows_of(d):
-        return pl.ds(pl.multiple_of(d * loc, loc), loc)
 
     def r_copy(d, target, sem):
-        view = gr.at[:, rows_of(d), :]
+        view = gr.at[d]
         return pltpu.make_async_remote_copy(
             src_ref=view, dst_ref=view, send_sem=sem, recv_sem=r_recv.at[d],
             device_id=(group, target), device_id_type=MESH)
 
     def n_copy(ch, d, target, sem):
-        view = gn.at[pl.ds(ch * per, per), rows_of(d), :]
+        view = gn.at[ch, d]
         return pltpu.make_async_remote_copy(
             src_ref=view, dst_ref=view, send_sem=sem, recv_sem=n_recv.at[ch, d],
             device_id=(group, target), device_id_type=MESH)
 
+    for k in order[:5]:
+        loads[k].wait()
     x = x_ref[...].astype(F32)
     center = jnp.mean(x, axis=-1, keepdims=True)
     spread = jnp.mean((x - center) ** 2, axis=-1, keepdims=True)
@@ -89,16 +93,16 @@
     n2 = jnp.concatenate(
         [normed[:half].reshape(half_rows, feat), normed[half:].reshape(half_rows, feat)], axis=1)
     n2_sc[...] = n2
-    own = rows_of(me)
-    gn[:, own, :] = n2.astype(BF).reshape(half, loc, lanes)
-
-    mask = mask_ref[...].astype(F32)
-    mask_pad = jnp.concatenate([mask, jnp.zeros((seqs, 128 - loc), F32)], axis=1)
-    mask_sq = jnp.concatenate([mask_pad, jnp.zeros((128 - seqs, 128), F32)], axis=0)
-    gr[tiles, own, :] = mask_sq.T[:loc].astype(BF)
+    gn[:, me] = n2.astype(BF).reshape(chunks, per, loc, lanes)
+
+    mask_pad = jnp.concatenate(
+        [mask_ref[...].astype(F32), jnp.zeros((loc, 128 - seqs), F32)], axis=1)
+    gr[me, tiles] = mask_pad.astype(BF)
+    mask_sq = jnp.concatenate([mask_pad, jnp.zeros((128 - loc, 128), F32)], axis=0).T
+    mask = mask_sq[:seqs]
     proj = jnp.concatenate(
         [former_ref[...].astype(F32), latter_ref[...].astype(F32),
-         jnp.zeros((feat, 128 - 2 * factor), F32)], axis=1).astype(BF)
+         jnp.zeros((128 - 2 * factor, feat), F32)], axis=0).astype(BF)
 
     def rows_for(i):
         packed = n2_sc[pl.ds(i, half, stride=loc), :]
@@ -107,7 +111,7 @@
 
     for i2 in range(pairs):
         rows = jnp.concatenate([rows_for(i2), rows_for(i2 + pairs)], axis=0).astype(BF)
-        both = mm(rows, proj)
+        both = lax.dot_general(rows, proj, NT, preferred_element_type=F32)
         lhs_sc[i2] = both.astype(BF)
         flipped = both.T
         rt_sc[pl.ds(i2 * factor, factor), :] = flipped[factor:2 * factor]
@@ -117,22 +121,23 @@
         b = rt_sc[pl.ds(2 * t + 1, pairs, stride=factor), :]
         top = jnp.where(low, a, pltpu.roll(b, seqs, 1))
         bottom = jnp.where(low, pltpu.roll(a, seqs, 1), b)
-        gr[t, own, :] = jnp.concatenate([top, bottom], axis=0).astype(BF)
-
-    wf_sc[...] = outw_ref[...].astype(F32)
-    for e in range(factor):
-        wl_sc[:, e * zdim:(e + 1) * zdim] = wf_sc[pl.ds(e, factor, stride=factor), :].astype(BF)
+        gr[me, t] = jnp.concatenate([top, bottom], axis=0).astype(BF)
 
     pl.semaphore_wait(barrier, nz + 1)
     r_copy(me, yside, ry_send.at[0]).start()
     for dz in range(1, nz):
         r_copy(me, dev(far(dz), yy, core), rz_send.at[dz]).start()
     r_copy(me, partner, rp_send.at[0, 0]).start()
+    n_copy(0, me, yside, ny_send.at[0, 0]).start()
     for ch in range(chunks):
         for dz in range(1, nz):
             n_copy(ch, me, dev(far(dz), yy, core), nz_send.at[ch, dz]).start()
 
-    stride = max(1, pairs // nz)
+    for k in order[5:11]:
+        loads[k].wait()
+    wf_sc[...] = outw_ref[...].astype(F32)
+    for e in range(factor):
+        wl_sc[:, e * zdim:(e + 1) * zdim] = wf_sc[pl.ds(e, factor, stride=factor), :].astype(BF)
 
     def r_relay(dz):
         d = dev(far(dz), yy, core)
@@ -149,26 +154,18 @@
                 part = res[:, (e - e0) * zdim:(e - e0 + 1) * zdim]
                 fold[i2, e * seqs:(e + 1) * seqs, :zdim] = part[:seqs]
                 fold[i2, e * seqs:(e + 1) * seqs, zdim:] = part[seqs:]
-        dz = (i2 + 1) // stride - 1
-
-        @pl.when((lax.rem(i2 + 1, stride) == 0) & (dz >= 1) & (dz < nz))
-        def _():
-            r_relay(dz)
-
         return carry
 
-    lax.fori_loop(0, pairs, fold_step, 0)
-    for dz in range(max(1, pairs // stride), nz):
-        r_relay(dz)
-    for ch in range(chunks):
-        n_copy(ch, me, yside, ny_send.at[ch, 0]).start()
+    lax.fori_loop(0, pairs // 2, fold_step, 0)
+    r_relay(1)
+    lax.fori_loop(pairs // 2, pairs, fold_step, 0)
+    r_relay(nz - 1)
 
     for i2 in range(pairs):
         for k in range(2):
             col = mask_sq[:, i2 + k * pairs:i2 + k * pairs + 1]
             mr_sc[i2, :, k * zdim:(k + 1) * zdim] = jnp.broadcast_to(col, (128, zdim)).astype(BF)
-    lw = jnp.concatenate([logitw_ref[...], jnp.zeros((zdim, 128 - heads), F32)], axis=1).T[:heads]
-    gw = lw * gain_ref[...]
+    gw = logitw_ref[...] * gain_ref[...]
     g0 = gw.astype(BF).astype(F32)
     g1 = (gw - g0).astype(BF).astype(F32)
     g2 = gw - g0 - g1
@@ -190,21 +187,21 @@
     switch = jnp.concatenate([switch, switch], axis=0)
     keep = iota(switch.shape, 0) // feat == (iota(switch.shape, 1) // width) % 2
     switch = jnp.where(keep, switch, 0.0).astype(BF)
-    fin = final_ref[...].astype(F32)
-    blocks = []
-    for h in range(heads):
-        blocks += [fin[h * width:(h + 1) * width]] * 2
-    fin = jnp.concatenate(blocks, axis=0)
-    fin = jnp.concatenate([fin, fin], axis=1)
-    keep = (iota(fin.shape, 0) // width) % 2 == iota(fin.shape, 1) // feat
+    fin = mm(final_ref[...], pick)
+    fin = jnp.concatenate([fin, fin], axis=0)
+    keep = iota(fin.shape, 0) // feat == (iota(fin.shape, 1) // width) % 2
     fin_sc[...] = jnp.where(keep, fin, 0.0).astype(BF)
 
+    for dz in range(2, nz - 1):
+        r_relay(dz)
+    for ch in range(1, chunks):
+        n_copy(ch, me, yside, ny_send.at[ch, 0]).start()
     for q in range(4):
         size = half_rows // 4
         pre = mm(n2_sc[q * size:(q + 1) * size, :].astype(BF), switch)
         gate_sc[q * size:(q + 1) * size, :] = jax.nn.sigmoid(pre)
 
-    for dz in range(nz):
+    for dz in [0, 1] + list(range(nz - 1, 1, -1)):
         d = dev(far(dz), 1 - yy, core)
         r_copy(d, partner, rp_send.at[1, dz]).wait_recv()
         r_copy(d, partner, rp_send.at[1, dz]).start()
@@ -214,16 +211,26 @@
         for dz in range(nz):
             d = dev(far(dz), lax.rem(yy + y, 2), 1 - core)
             r_copy(d, partner, rp_send.at[y, dz]).wait_recv()
-    load.wait()
+    for k in order[-2:]:
+        loads[k].wait()
 
     real = tok_ref[...] == 1
     mean_of = jnp.full((zdim, zdim), 1.0 / zdim, F32).astype(BF)
     rel = pairs // chunks
 
+    def n_relay(ch):
+        for dz in range(1, nz):
+            d = dev(far(dz), yy, core)
+            n_copy(ch, d, yside, ny_send.at[ch, dz]).wait_recv()
+            n_copy(ch, d, yside, ny_send.at[ch, dz]).start()
+            n_copy(ch, d, partner, np_send.at[ch, 0, dz]).start()
+
+    n_relay(0)
+
     def pair_step(i2, carry):
-        lhs = jnp.concatenate([gr[t] for t in range(tiles)], axis=1)
+        lhs = jnp.concatenate([gr[:, t].reshape(span, 128) for t in range(tiles)], axis=1)
         acc = mm(lhs, fold[i2])
-        counts = mm(gr[tiles], mr_sc[i2])
+        counts = mm(gr[:, tiles].reshape(span, 128), mr_sc[i2])
         acc = acc / (1.0 + counts)
         for k in range(2):
             i = i2 + k * pairs
@@ -244,13 +251,9 @@
                 lg_sc[t, pl.ds(i, heads, stride=loc), :] = logits[:, t * 128:(t + 1) * 128]
         ch = i2 // rel
 
-        @pl.when(lax.rem(i2, rel) == 0)
+        @pl.when((lax.rem(i2, rel) == 0) & (ch + 1 < chunks))
         def _():
-            for dz in range(1, nz):
-                d = dev(far(dz), yy, core)
-                n_copy(ch, d, yside, ny_send.at[ch, dz]).wait_recv()
-                n_copy(ch, d, yside, ny_send.at[ch, dz]).start()
-                n_copy(ch, d, partner, np_send.at[ch, 0, dz]).start()
+            n_relay(ch + 1)
 
         @pl.when(lax.rem(i2, rel) == rel - 1)
         def _():
@@ -262,8 +265,6 @@
         return carry
 
     lax.fori_loop(0, pairs, pair_step, 0)
-    save = pltpu.make_async_copy(pair_new, pair_out_hbm, out_sem)
-    save.start()
 
     logits = jnp.concatenate([lg_sc[t] for t in range(span // 128)], axis=1)
     top = jnp.max(logits, axis=1, keepdims=True)
@@ -277,7 +278,7 @@
                 n_copy(ch, d, partner, np_send.at[ch, y, dz]).wait_recv()
         for q in range(0, per, 2):
             p = ch * per + q
-            rhs = jnp.concatenate([gn[p], gn[p + 1]], axis=1)
+            rhs = jnp.concatenate([gn[ch, :, q + k].reshape(span, lanes) for k in range(2)], axis=1)
             res = mm(weights, rhs).astype(BF)
             for k in range(2):
                 at = pl.ds(pl.multiple_of((p + k) * loc, loc), loc)
@@ -291,7 +292,8 @@
         for g in range(2):
             mean = mm(a2_sc[at, g * rows:(g + 1) * rows], bd_sc[g])
             gated = (gate_sc[at, g * wide:(g + 1) * wide] * mean).astype(BF)
-            total += mm(gated, fin_sc[g * wide:(g + 1) * wide, :])
+            total += lax.dot_general(
+                gated, fin_sc[:, g * wide:(g + 1) * wide], NT, preferred_element_type=F32)
         for k in range(2):
             where = pl.ds(ch * per + k * half, per)
             piece = total[:, k * feat:(k + 1) * feat].reshape(per, loc, feat)
@@ -317,7 +319,6 @@
         return carry
 
     lax.fori_loop(0, chunks, drain, 0)
-    save.wait()
 
 
 def shards(row_count, x, pair, mask, tok, scale, former, latter, outw, gain, logitw, content, switch, final):
@@ -333,16 +334,20 @@
     pairs = loc // 2
     tiles = factor * seqs // 128
     vm = pl.BlockSpec(memory_space=pltpu.VMEM)
-    hbm = pl.BlockSpec(memory_space=pl.ANY)
+    hbm = pl.BlockSpec(memory_space=pltpu.MemorySpace.HBM)
     dma = pltpu.SemaphoreType.DMA
+    operands = (
+        x, pair, mask.T, tok.reshape(1, span), scale.reshape(1, feat), former.T, latter.T, outw,
+        gain.reshape(1, zdim), logitw.T, content, switch, final.T)
+    operands = tuple(pltpu.with_memory_space_constraint(a, pltpu.MemorySpace.HBM) for a in operands)
     return pl.pallas_call(
         functools.partial(kernel, (nz, chunks)),
         out_shape=(jax.ShapeDtypeStruct(x.shape, x.dtype), jax.ShapeDtypeStruct(pair.shape, pair.dtype)),
-        in_specs=[vm, hbm] + [vm] * 11,
-        out_specs=(vm, hbm),
-        scratch_shapes=[
-            pltpu.VMEM((tiles + 1, span, 128), BF),
-            pltpu.VMEM((half, span, lanes), BF),
+        in_specs=[hbm] * 13,
+        out_specs=(vm, vm),
+        scratch_shapes=[pltpu.VMEM(a.shape, a.dtype) for a in operands] + [
+            pltpu.VMEM((row_count, tiles + 1, loc, 128), BF),
+            pltpu.VMEM((chunks, row_count, half // chunks, loc, lanes), BF),
             pltpu.VMEM((pairs, factor * seqs, 2 * zdim), BF),
             pltpu.VMEM((half * loc, lanes), F32),
             pltpu.VMEM((pairs, 2 * seqs, 128), BF),
@@ -353,11 +358,9 @@
             pltpu.VMEM((4 * heads, 4 * zdim), BF),
             pltpu.VMEM((span // 128, heads * loc, 128), F32),
             pltpu.VMEM((2, heads * lanes // 2, heads * width), BF),
-            pltpu.VMEM((2 * heads * width, lanes), BF),
+            pltpu.VMEM((lanes, 2 * heads * width), BF),
             pltpu.VMEM((half * loc, 2 * heads * width), F32),
             pltpu.VMEM((half * loc, heads * lanes), BF),
-            pltpu.VMEM((loc, span, zdim), BF),
-            pltpu.VMEM((loc, span, zdim), BF),
             dma((row_count,)),
             dma((nz,)),
             dma((nz,)),
@@ -366,14 +369,12 @@
             dma((chunks, nz)),
             dma((chunks, nz)),
             dma((chunks, 2, nz)),
-            dma,
-            dma,
+            dma((13,)),
         ],
         compiler_params=pltpu.CompilerParams(
-            collective_id=0, has_side_effects=True, vmem_limit_bytes=60 * 1024 * 1024),
+            collective_id=0, has_side_effects=True, vmem_limit_bytes=32 * 1024 * 1024),
         name="msa_step",
-    )(x, pair, mask, tok.reshape(1, span), scale.reshape(1, feat), former, latter, outw,
-      gain.reshape(1, zdim), logitw, content, switch, final)
+    )(*operands)
 
 
 def solution(mesh):

time: 55.9 us -> 40.9 us (0.73)
  the two profiles are of different devices: /device:TPU:10 before, /device:TPU:9 now
where the time goes in v2:
time: 40.9 us; the launch traced here: 40.7 us
  Pallas kernels  38.4 us (94%)
  local copies, waits for them, and re-layouts  1.67 us (4%)
  between operations  0.64 us (2%)
    pallas_call x1, Pallas kernels, shards(): pl.pallas_call(functools.partial(kernel, (nz, chunks)), out_shape=(jax.Sh...  38.4 us
    unnamed x2, local copies, waits for them, and re-layouts  1.67 us

profile of v2, /device:TPU:9, one launch (start us, length us, event | category | flops | bytes accessed | tf_op | source)
XLA Modules:
  0.0 40.7 jit_solution(881212933384226180)
XLA Ops:
  0.6 38.4 %msa_step.1 = (bf16[64,16,64]{2,1,0:T(8,128)(2,1)S(1)}, bf16[16,256,128]{2,1,0:T(8,128)(2,1)S(1)}) custom-call(bf16[64,16,64]{2,1,0:T(8,128)(2,1)} %refs_0_.1, bf16[16,256,128]{2,1,0:T(8,128)(2,1)} %refs_1_.1, s32[16,64]{1,0:T(8,128)} %bitcast.9, s32[1,256]{1,0:T(1,128)} %bitcast.13, f32[1,64]{1,0:T(1,128)} %bitcast.14, bf16[32,64]{1,0:T(8,128)(2,1)} %bitcast.10, ...), custom_call_target="tpu_custom_call" | custom-call | tf_op jit(solution)/shard_map/msa_step/pallas_call | solution.py:343
  39.1 0.7 %copy.17 = bf16[64,16,64]{2,1,0:T(8,128)(2,1)} copy(bf16[64,16,64]{2,1,0:T(8,128)(2,1)S(1)} %get-tuple-element.4) | data formatting | bytes 262144
  39.8 1.0 %copy.18 = bf16[16,256,128]{2,1,0:T(8,128)(2,1)} copy(bf16[16,256,128]{2,1,0:T(8,128)(2,1)S(1)} %get-tuple-element.5) | data formatting | bytes 2097152

commit v3 on v2

--- a/solution.py
+++ b/solution.py
@@ -328,7 +328,7 @@
     heads = logitw.shape[1]
     width = content.shape[1] // heads
     nz = row_count // 4
-    chunks = 4
+    chunks = 2
     half = seqs // 2
     lanes = 2 * feat
     pairs = loc // 2

time: 40.9 us -> 38.8 us (0.949)
  Pallas kernels: 38.4 us -> 36.3 us
    pallas_call x1, Pallas kernels: 38.4 us -> 36.3 us  [shards(): pl.pallas_call(functools.partial(kernel, (nz, chunks)), out_shape=(jax.Sh...]
where the time goes in v3:
time: 38.8 us; the launch traced here: 38.6 us
  Pallas kernels  36.3 us (94%)
  local copies, waits for them, and re-layouts  1.67 us (4%)
  between operations  0.64 us (2%)
    pallas_call x1, Pallas kernels, shards(): pl.pallas_call(functools.partial(kernel, (nz, chunks)), out_shape=(jax.Sh...  36.3 us
    unnamed x2, local copies, waits for them, and re-layouts  1.67 us

profile of v3, /device:TPU:9, one launch (start us, length us, event | category | flops | bytes accessed | tf_op | source)
XLA Modules:
  0.0 38.6 jit_solution(8734412893310101505)
XLA Ops:
  0.6 36.3 %msa_step.1 = (bf16[64,16,64]{2,1,0:T(8,128)(2,1)S(1)}, bf16[16,256,128]{2,1,0:T(8,128)(2,1)S(1)}) custom-call(bf16[64,16,64]{2,1,0:T(8,128)(2,1)} %refs_0_.1, bf16[16,256,128]{2,1,0:T(8,128)(2,1)} %refs_1_.1, s32[16,64]{1,0:T(8,128)} %bitcast.9, s32[1,256]{1,0:T(1,128)} %bitcast.13, f32[1,64]{1,0:T(1,128)} %bitcast.14, bf16[32,64]{1,0:T(8,128)(2,1)} %bitcast.10, ...), custom_call_target="tpu_custom_call" | custom-call | tf_op jit(solution)/shard_map/msa_step/pallas_call | solution.py:343
  37.0 0.7 %copy.17 = bf16[64,16,64]{2,1,0:T(8,128)(2,1)} copy(bf16[64,16,64]{2,1,0:T(8,128)(2,1)S(1)} %get-tuple-element.4) | data formatting | bytes 262144
  37.7 1.0 %copy.18 = bf16[16,256,128]{2,1,0:T(8,128)(2,1)} copy(bf16[16,256,128]{2,1,0:T(8,128)(2,1)S(1)} %get-tuple-element.5) | data formatting | bytes 2097152
